TPU v7x, 128 devices: a whole 4x4x4 slice. The times are simulated.
128 devices in a mesh: ctx: 16 (over z, y), head: 8 (over x, core).
Axes of the slice: x: 4, y: 4, z: 4, core: 2. Of those that a mesh axis runs over, the one named last changes fastest.
Arguments:
- queries: bfloat16 [16384, 12288], P('ctx', 'head'), may hold values from -24 to 24
- key_rows: bfloat16 [16384, 768], P('ctx'), may hold values from -6 to 6
- value_rows: bfloat16 [16384, 512], P('ctx'), may hold values from -6 to 6
- comp_key_weight: float32 [32, 768], replicated, may hold values from 0.35355338 to 0.70710677
- comp_value_weight: float32 [32, 512], replicated, may hold values from 0.17677669 to 0.53033006
- block_picks: int32 [64, 4, 16], P('ctx'), may hold values from 0 to 252, as said below
- gate_logits: float32 [16384, 3, 64], P('ctx', None, 'head'), may hold values from -6 to 6
- out_weight: bfloat16 [8192, 2560], P('head'), may hold values from -0.25 to 0.25
Outputs:
- layer_out: bfloat16 [16384, 2560], P(('ctx', 'head'))
Inputs may be any that keep to these rules, and one draw needn't show every extreme that they name: `block_picks`: for each group, the lists of the 256-position query blocks held by one ctx shard name exactly 1024 / 256 distinct blocks of each earlier shard and of their own shard, and none of later shards; the own-shard blocks named are the first blocks of those query blocks. Every list names the first block of its own query block. Names may repeat within a list.
All inputs are finite; a program needn't handle non-finite values.
Results may differ from a plain program's by a relative error of at most 0.03.
Values may be sent and summed in bfloat16 or wider, within the bound.
A program may use at most 128 MiB of HBM per device.

v0:
```python
import jax
import jax.numpy as jnp
from jax import lax
from jax.sharding import PartitionSpec as P

HEADS = 64
GROUPS = 4
QUERY_KEY_WIDTH = 192
DV = 128
CBLK = 32
KBLK = 64
PICKS = 16
WINDOW = 512
QBLK = 256
NEG_FILL = -1e30


def shifted(block, axis, distance):
    devices = range(lax.axis_size(axis))
    route = [(i - distance, i) for i in devices if i - distance in devices]
    return lax.ppermute(block, axis, route)


def softmax_parts(scores, keep_mask):
    row_top = jnp.max(jnp.where(keep_mask, scores, NEG_FILL), axis=-1, keepdims=True)
    weights = jnp.where(keep_mask, jnp.exp(scores - row_top), 0.0)
    return (weights.astype(jnp.bfloat16), jnp.sum(weights, axis=-1))


def local(
    queries,
    key_rows,
    value_rows,
    comp_key_weight,
    comp_value_weight,
    block_picks,
    gate_logits,
    out_weight,
):
    tok_rows = queries.shape[0]
    heads_here = queries.shape[1] // QUERY_KEY_WIDTH
    shard_index = lax.axis_index("ctx")
    group_index = lax.axis_index("head") * heads_here // (HEADS // GROUPS)
    lane_count = QUERY_KEY_WIDTH + DV
    per_owner = tok_rows // KBLK
    query_blocks = tok_rows // QBLK
    score_scale = QUERY_KEY_WIDTH ** (-0.5)
    own_keys = lax.dynamic_slice_in_dim(key_rows, group_index * QUERY_KEY_WIDTH, QUERY_KEY_WIDTH, 1)
    own_values = lax.dynamic_slice_in_dim(value_rows, group_index * DV, DV, 1)
    packed = jnp.concatenate([own_keys, own_values], axis=1).reshape(per_owner, KBLK * lane_count)
    query_heads = queries.reshape(tok_rows, heads_here, QUERY_KEY_WIDTH)
    block_queries = queries.reshape(query_blocks, QBLK, heads_here, QUERY_KEY_WIDTH)
    positions = shard_index * tok_rows + jnp.arange(tok_rows, dtype=jnp.int32)
    query_pos = positions.reshape(query_blocks, QBLK)
    gates = jax.nn.sigmoid(gate_logits)
    key_weight = lax.dynamic_slice_in_dim(
        comp_key_weight, group_index * QUERY_KEY_WIDTH, QUERY_KEY_WIDTH, 1
    )
    value_weight = lax.dynamic_slice_in_dim(comp_value_weight, group_index * DV, DV, 1)
    comp_keys = jnp.sum(
        own_keys.reshape(tok_rows // CBLK, CBLK, QUERY_KEY_WIDTH).astype(jnp.float32)
        * key_weight[None],
        axis=1,
    ).astype(jnp.bfloat16)
    comp_values = jnp.sum(
        own_values.reshape(tok_rows // CBLK, CBLK, DV).astype(jnp.float32) * value_weight[None],
        axis=1,
    ).astype(jnp.bfloat16)
    all_comp_keys, all_comp_values = (
        lax.all_gather(comp_keys, "ctx", axis=0, tiled=True),
        lax.all_gather(comp_values, "ctx", axis=0, tiled=True),
    )
    comp_count = all_comp_keys.shape[0]
    comp_ends = (jnp.arange(comp_count, dtype=jnp.int32) + 1) * CBLK - 1
    row_span = min(512, tok_rows)

    def comp_span(span_index):
        first_row = span_index * row_span
        span_queries = lax.dynamic_slice_in_dim(query_heads, first_row, row_span, 0)
        span_pos = lax.dynamic_slice_in_dim(positions, first_row, row_span, 0)
        scores = (
            jnp.einsum(
                "thc,nc->thn", span_queries, all_comp_keys, preferred_element_type=jnp.float32
            )
            * score_scale
        )
        keep_mask = comp_ends[None, None, :] <= span_pos[:, None, None]
        weights, weight_sum = softmax_parts(scores, keep_mask)
        span_out = jnp.einsum(
            "thn,nd->thd", weights, all_comp_values, preferred_element_type=jnp.float32
        )
        return span_out / jnp.maximum(weight_sum, 1.0)[..., None]

    comp_out = lax.map(comp_span, jnp.arange(tok_rows // row_span, dtype=jnp.int32)).reshape(
        tok_rows, heads_here, DV
    )
    rim_rows = shifted(packed[per_owner - WINDOW // KBLK :], "ctx", 1)
    extended = jnp.concatenate([rim_rows, packed], axis=0).reshape(WINDOW + tok_rows, lane_count)
    window_spans = jnp.stack(
        [
            extended[span_index * QBLK : span_index * QBLK + WINDOW + QBLK]
            for span_index in range(query_blocks)
        ]
    )
    win_scores = (
        jnp.einsum(
            "bqhc,bkc->bqhk",
            block_queries,
            window_spans[..., :QUERY_KEY_WIDTH],
            preferred_element_type=jnp.float32,
        )
        * score_scale
    )
    key_pos = (
        shard_index * tok_rows
        - WINDOW
        + jnp.arange(query_blocks, dtype=jnp.int32)[:, None] * QBLK
        + jnp.arange(WINDOW + QBLK, dtype=jnp.int32)[None, :]
    )
    keep_mask = (
        (key_pos[:, None, :] >= 0)
        & (key_pos[:, None, :] <= query_pos[:, :, None])
        & (key_pos[:, None, :] >= query_pos[:, :, None] - WINDOW)
    )
    win_weights, win_sum = softmax_parts(win_scores, keep_mask[:, :, None, :])
    win_out = (
        jnp.einsum(
            "uzai,uix->uzax",
            win_weights,
            window_spans[..., QUERY_KEY_WIDTH:],
            preferred_element_type=jnp.float32,
        )
        / win_sum[..., None]
    )
    my_picks = lax.dynamic_index_in_dim(block_picks, group_index, 1, keepdims=False)
    flat_picks = my_picks.reshape(query_blocks * PICKS)
    gathered = lax.all_gather(packed, "ctx", axis=0, tiled=True)
    tiled_row_groups = gathered[flat_picks]
    tiled_row_groups = tiled_row_groups.reshape(query_blocks, PICKS * KBLK, lane_count)
    pick_order = jnp.arange(PICKS, dtype=jnp.int32)
    repeated = jnp.any(
        (my_picks[:, :, None] == my_picks[:, None, :])
        & (pick_order[None, None, :] < pick_order[None, :, None]),
        axis=-1,
    )
    pick_pos = (my_picks[:, :, None] * KBLK + jnp.arange(KBLK, dtype=jnp.int32)).reshape(
        query_blocks, PICKS * KBLK
    )
    live_mask = jnp.repeat(jnp.logical_not(repeated), KBLK, axis=1)
    keep_mask = (pick_pos[:, None, :] <= query_pos[:, :, None]) & live_mask[:, None, :]
    sel_scores = (
        jnp.einsum(
            "bqhc,bkc->bqhk",
            block_queries,
            tiled_row_groups[..., :QUERY_KEY_WIDTH],
            preferred_element_type=jnp.float32,
        )
        * score_scale
    )
    selected_weights, selected_sum = softmax_parts(sel_scores, keep_mask[:, :, None, :])
    sel_out = (
        jnp.einsum(
            "uzai,uix->uzax",
            selected_weights,
            tiled_row_groups[..., QUERY_KEY_WIDTH:],
            preferred_element_type=jnp.float32,
        )
        / selected_sum[..., None]
    )
    mixed = (
        gates[:, 0, :, None] * comp_out
        + gates[:, 1, :, None] * sel_out.reshape(tok_rows, heads_here, DV)
        + gates[:, 2, :, None] * win_out.reshape(tok_rows, heads_here, DV)
    )
    attended = mixed.astype(jnp.bfloat16).reshape(tok_rows, heads_here * DV)
    return lax.psum_scatter(
        jnp.dot(attended, out_weight, preferred_element_type=jnp.float32).astype(jnp.bfloat16),
        "head",
        scatter_dimension=0,
        tiled=True,
    )


def solution(mesh):
    placed = (
        P("ctx", "head"),
        P("ctx", None),
        P("ctx", None),
        P(),
        P(),
        P("ctx", None, None),
        P("ctx", None, "head"),
        P("head", None),
    )
    return jax.shard_map(
        local, mesh=mesh, in_specs=placed, out_specs=P(("ctx", "head"), None), check_vma=False
    )
```

profile of v0, /device:TPU:0, one launch (start us, length us, event | category | flops | bytes accessed | tf_op | source)
XLA Modules:
  0.0 297.9 jit_solution(15637494506940244456)
XLA Ops:
  13.0 4.3 %collective-permute-start = (bf16[8,20480]{1,0:T(8,128)(2,1)}, bf16[8,20480]{1,0:T(8,128)(2,1)}, u32[]{:S(2)}, u32[]{:S(2)}) collective-permute-start(bf16[8,20480]{1,0:T(8,128)(2,1)} %slice.53), channel_id=1, source_target_pairs={{0,8},{8,16},{16,24},{24,32},{32,40},{40,48},{48,56},{56,64},{64,7... | collective-permute-start | bytes 983048 | tf_op jit(solution)/shard_map/ppermute | solution.py:21
  26.5 3.2 %copy.73 = bf16[1024,1536]{0,1:T(8,128)(2,1)S(1)} copy(bf16[1024,1536]{1,0:T(8,128)(2,1)} %param.10) | data formatting | bytes 6291456 | tf_op args[0]
  32.0 26.6 %all_gather.9 = bf16[512,192]{1,0:T(8,128)(2,1)} all-gather(bf16[32,192]{1,0:T(8,128)(2,1)S(1)} %multiply_reduce_fusion), channel_id=1, replica_groups=mesh['ctx'=16,'head'=8] {'ctx'}, dimensions={0}, use_global_device_ids=true | all-gather | bytes 208896 | tf_op jit(solution)/shard_map/all_gather | solution.py:70
  61.5 22.6 %all_gather.10 = bf16[512,128]{1,0:T(8,128)(2,1)S(1)} all-gather(bf16[32,128]{1,0:T(8,128)(2,1)S(1)} %multiply_reduce_fusion.1), channel_id=1, replica_groups=mesh['ctx'=16,'head'=8] {'ctx'}, dimensions={0}, use_global_device_ids=true | all-gather | bytes 139264 | tf_op jit(solution)/shard_map/all_gather | solution.py:71
  86.2 3.0 compare_and_fusion.1
  89.6 30.3 %while.11 = (s32[]{:T(128)}, f32[2,512,8,128]{3,2,1,0:T(8,128)}, s32[2]{0:T(128)}, s32[1024]{0:T(1024)}, bf16[1024,8,192]{0,2,1:T(8,128)(2,1)S(1)}, /*index=5*/b...) while((s32[]{:T(128)}, f32[2,512,8,128]{3,2,1,0:T(8,128)}, ...), condition=%wide.region_5.6_spmd.clone, body=%wide.region_2.5_spmd.clone.sunk | while | flops 1357649920 | bytes 33974984 | solution.py:94
  93.2 5.5 %fusion.113 = (f32[512,8]{0,1:T(8,128)S(1)}, bf16[512,8,512]{0,2,1:T(8,128)(2,1)}) fusion(f32[512,8,512]{0,2,1:T(8,128)S(1)} %fusion.112, pred[512,512]{0,1:T(8,128)(4,1)S(1)} %broadcast_compare_fusion.3), kind=kOutput, calls=%fused_computation.122.clone.1 | output fusion | flops 14680575 | bytes 12861440 | tf_op jit(solution)/shard_map/while/body/eval_jaxpr/sub | solution.py:26
  98.8 3.4 %divide_bitcast_fusion.2 = f32[1,512,8,128]{3,1,2,0:T(8,128)S(1)} fusion(bf16[512,8,512]{0,2,1:T(8,128)(2,1)} %get-tuple-element.158, f32[512,8]{0,1:T(8,128)S(1)} %broadcast_maximum_fusion.2, bf16[512,128]{1,0:T(8,128)(2,1)S(1)} %get-tuple-element.188), kind=kOutput, calls=%fused_computation.13.clone.1 | convolution fusion | flops 537395200 | bytes 6438912 | tf_op jit(solution)/shard_map/while/body/eval_jaxpr/thn,nd->thd/dot_general | solution.py:89
  108.4 5.5 %fusion.113 = (f32[512,8]{0,1:T(8,128)S(1)}, bf16[512,8,512]{0,2,1:T(8,128)(2,1)}) fusion(f32[512,8,512]{0,2,1:T(8,128)S(1)} %fusion.112, pred[512,512]{0,1:T(8,128)(4,1)S(1)} %broadcast_compare_fusion.3), kind=kOutput, calls=%fused_computation.122.clone.1 | output fusion | flops 14680575 | bytes 12861440 | tf_op jit(solution)/shard_map/while/body/eval_jaxpr/sub | solution.py:26
  113.9 3.4 %divide_bitcast_fusion.2 = f32[1,512,8,128]{3,1,2,0:T(8,128)S(1)} fusion(bf16[512,8,512]{0,2,1:T(8,128)(2,1)} %get-tuple-element.158, f32[512,8]{0,1:T(8,128)S(1)} %broadcast_maximum_fusion.2, bf16[512,128]{1,0:T(8,128)(2,1)S(1)} %get-tuple-element.188), kind=kOutput, calls=%fused_computation.13.clone.1 | convolution fusion | flops 537395200 | bytes 6438912 | tf_op jit(solution)/shard_map/while/body/eval_jaxpr/thn,nd->thd/dot_general | solution.py:89
  120.6 3.9 %reshape.229 = bf16[4,256,8,192]{1,0,3,2:T(4,128)(2,1)} reshape(bf16[1024,1536]{0,1:T(8,128)(2,1)S(1)} %bitcast.144) | data formatting | bytes 6291456 | tf_op jit(solution)/shard_map/reshape | solution.py:52
  127.8 3.3 %compare_and_fusion = pred[4,256,1024]{1,2,0:T(8,128)(4,1)} fusion(s32[4,256]{1,0:T(4,128)S(1)} %copy-done.8, s32[4,1024]{1,0:T(4,128)S(1)} %broadcast_add_fusion, pred[4,1024]{1,0:T(4,128)(4,1)S(1)} %and.51), kind=kLoop, calls=%fused_computation.55 | loop fusion | flops 2097152 | bytes 1073152 | tf_op jit(solution)/shard_map/and | solution.py:150
  144.0 3.0 pad_maximum_fusion
  147.0 15.6 %fusion.88 = (f32[4,256,8]{1,2,0:T(8,128)S(1)}, bf16[4,256,8,768]{1,3,2,0:T(8,128)(2,1)}) fusion(pred[4,256,768]{1,2,0:T(8,128)(4,1)} %compare_and_fusion.1, bf16[4,256,8,192]{1,0,3,2:T(4,128)(2,1)S(1)} %copy-done.2, bf16[4,768,320]{1,2,0:T(8,128)(2,1)} %pad_maximum_fusion), kind=kOutput, calls=%fused_computation.124 | convolution fusion | flops 4875878912 | bytes 22839296 | tf_op jit(solution)/shard_map/sub | solution.py:26
  162.6 7.8 %broadcast_divide_fusion = f32[4,256,8,128]{3,1,2,0:T(8,128)S(1)} fusion(f32[4,256,8]{1,2,0:T(8,128)S(1)} %get-tuple-element.103, bf16[4,256,8,768]{1,3,2,0:T(8,128)(2,1)} %get-tuple-element.104, bf16[1,768,320]{1,2,0:T(8,128)(2,1)} %get-tuple-element.99, bf16[1,768,320]{1,2,0:T(8,128)(2,1)} %get-tuple-element.98, bf16[1,768,320]{1,2,0:T(8,128)(2,1)} %copy.90, ...), kind=kOutput, calls=%fused_computation.61 | convolution fusion | flops 1614807040 | bytes 18776064 | tf_op jit(solution)/shard_map/uzai,uix->uzax/dot_general | solution.py:127
  170.4 4.5 %copy.94 = f32[4,256,8,128]{3,2,1,0:T(8,128)} copy(f32[4,256,8,128]{3,1,2,0:T(8,128)S(1)} %broadcast_divide_fusion) | data formatting | bytes 8388608 | tf_op jit(solution)/shard_map/div | solution.py:127
  174.9 9.8 %gather_fusion = bf16[64,20480]{1,0:T(8,128)(2,1)S(1)} fusion(bf16[256,20480]{1,0:T(8,128)(2,1)} %all-gather.2.cloned.1.call-done, s32[1024]{0:T(1024)S(1)} %pad_clamp_fusion), kind=kCustom, calls=%fused_computation | custom fusion | bytes 5243136 | tf_op jit(solution)/shard_map/gather | solution.py:138
  184.7 4.7 %reshape.228 = bf16[4,1024,320]{2,1,0:T(8,128)(2,1)} reshape(bf16[64,20480]{1,0:T(8,128)(2,1)S(1)} %gather_fusion) | data formatting | bytes 5242880 | tf_op jit(solution)/shard_map/reshape | solution.py:139
  189.4 20.7 %fusion.93 = (f32[4,256,8]{1,2,0:T(8,128)S(1)}, bf16[4,256,8,1024]{1,3,2,0:T(8,128)(2,1)}) fusion(pred[4,256,1024]{1,2,0:T(8,128)(4,1)} %compare_and_fusion, bf16[4,256,8,192]{1,0,3,2:T(4,128)(2,1)} %reshape.229, bf16[4,1024,320]{2,1,0:T(8,128)(2,1)} %reshape.228), kind=kOutput, calls=%fused_computation.125 | convolution fusion | flops 6501172224 | bytes 29392896 | tf_op jit(solution)/shard_map/sub | solution.py:26
  210.2 11.4 %fusion.46 = f32[4,256,8,128]{3,1,2,0:T(8,128)S(1)} fusion(bf16[4,256,8,1024]{1,3,2,0:T(8,128)(2,1)} %get-tuple-element.106, f32[4,256,8]{1,2,0:T(8,128)S(1)} %get-tuple-element.105, bf16[4,1024,320]{2,1,0:T(8,128)(2,1)} %reshape.228), kind=kOutput, calls=%fused_computation.58 | convolution fusion | flops 2148532224 | bytes 22052864 | tf_op jit(solution)/shard_map/uzai,uix->uzax/dot_general | solution.py:162
  221.6 4.4 %copy.86 = f32[4,256,8,128]{3,2,1,0:T(8,128)} copy(f32[4,256,8,128]{3,1,2,0:T(8,128)S(1)} %fusion.46) | data formatting | bytes 8388608 | tf_op jit(solution)/shard_map/div | solution.py:162
  228.3 3.0 %mul.146 = f32[1024,8,128]{2,1,0:T(8,128)} broadcast(f32[1024,8]{1,0:T(8,128)S(1)} %copy-done.5), dimensions={0,1} | broadcast | bytes 4227072 | tf_op jit(solution)/shard_map/mul | solution.py:173
  231.3 19.5 %convolution_convert_fusion = bf16[1024,2560]{1,0:T(8,128)(2,1)} fusion(bf16[1024,2560]{1,0:T(8,128)(2,1)} %param.17, f32[128,8,8,128]{3,2,1,0:T(8,128)} %bitcast.148, f32[128,8,8,128]{3,2,1,0:T(8,128)} %bitcast.147, f32[128,8,8,128]{3,2,1,0:T(8,128)} %bitcast.149, f32[128,8,8,128]{3,2,1,0:T(8,128)S(1)} %bitcast.146, f32[128,8,8,128]{3,2,1,0:T(8,128)} %bitcast.32, ...), kind=kOutput, calls=%fused_computation.48 | convolution fusion | flops 5377622016 | bytes 35651584 | tf_op jit(solution)/shard_map/dot_general | solution.py:177
  250.8 39.7 %reduce-scatter.2.cloned.1.call-done = bf16[128,2560]{1,0:T(8,128)(2,1)} async-done(((bf16[1024,2560]{1,0:T(8,128)(2,1)}), bf16[128,2560]{1,0:T(8,128)(2,1)}) %reduce-scatter.2.cloned.1.call-update) | async-done | bytes 655376 | tf_op jit(solution)/shard_map/reduce_scatter | solution.py:176
  (98 shorter events, 53.6 us)
Async XLA Ops:
  6.5 1.4 copy-start
  6.5 168.4 %all-gather.2.cloned.1.call-start = ((), (), s32[]{:S(2)}) async-start(), calls=%async_computation.1 | async-start | bytes 11141120 | tf_op jit(solution)/shard_map/all_gather | solution.py:137
  11.6 278.9 %reduce-scatter.2.cloned.1.call-start = ((), (), s32[]{:S(2)}) async-start(), calls=%async_computation.2 | async-start | bytes 5898240 | tf_op jit(solution)/shard_map/reduce_scatter | solution.py:176
  13.0 118.0 %collective-permute-start = (bf16[8,20480]{1,0:T(8,128)(2,1)}, bf16[8,20480]{1,0:T(8,128)(2,1)}, u32[]{:S(2)}, u32[]{:S(2)}) collective-permute-start(bf16[8,20480]{1,0:T(8,128)(2,1)} %slice.53), channel_id=1, source_target_pairs={{0,8},{8,16},{16,24},{24,32},{32,40},{40,48},{48,56},{56,64},{64,7... | collective-permute-start | bytes 983048 | tf_op jit(solution)/shard_map/ppermute | solution.py:21
  91.5 1.4 copy-start.7
  106.6 1.5 copy-start.7
  120.0 4.6 %copy-start.9 = (pred[4,16]{1,0:T(4,128)(4,1)S(1)}, pred[4,16]{1,0:T(4,128)(4,1)}, u32[]{:S(2)}) copy-start(pred[4,16]{1,0:T(4,128)(4,1)} %and_reduce_fusion) | copy-start | bytes 196
  120.0 4.7 %copy-start.6 = (f32[1024,8]{0,1:T(8,128)S(1)}, f32[1024,8]{0,1:T(8,128)}, u32[]{:S(2)}) copy-start(f32[1024,8]{0,1:T(8,128)} %get-tuple-element.100) | copy-start | bytes 98308
  120.0 7.8 %copy-start.8 = (s32[4,256]{1,0:T(4,128)S(1)}, s32[4,256]{1,0:T(4,128)}, u32[]{:S(2)}) copy-start(s32[4,256]{1,0:T(4,128)} %add_add_fusion) | copy-start | bytes 12292
  134.5 12.5 %copy-start.2 = (bf16[4,256,8,192]{1,0,3,2:T(4,128)(2,1)S(1)}, bf16[4,256,8,192]{1,0,3,2:T(4,128)(2,1)}, u32[]{:S(2)}) copy-start(bf16[4,256,8,192]{1,0,3,2:T(4,128)(2,1)} %reshape.229) | copy-start | bytes 9437188
  221.6 4.5 %copy-start.3 = (f32[1024,8]{1,0:T(8,128)S(1)}, f32[1024,8]{1,0:T(8,128)}, u32[]{:S(2)}) copy-start(f32[1024,8]{1,0:T(8,128)} %copy.72) | copy-start | bytes 98308
  226.0 1.1 copy-start.4
  226.0 2.3 copy-start.5
  231.3 59.2 %copy-start.1 = (bf16[1024,768]{1,0:T(8,128)(2,1)S(1)}, bf16[1024,768]{1,0:T(8,128)(2,1)}, u32[]{:S(2)}) copy-start(bf16[1024,768]{1,0:T(8,128)(2,1)} %param.11) | copy-start | bytes 4718596
Sparse Core Ops, SparseCore 0:
  11.7 84.1 all-gather.1
  250.9 39.5 reduce-scatter.1
where the time goes:
time: 302 us; the launch traced here: 298 us
  matrix products  84.8 us (28%)
  local copies, waits for them, and re-layouts  74 us (25%)
  blocking collectives  49.2 us (16%)
  waiting for transfers between devices  39.7 us (13%)
  other arithmetic  30.4 us (10%)
  between operations  14.1 us (5%)
  starting transfers between devices  4.33 us (1%)
    reduce_scatter x1, waiting for transfers between devices, local(): lax.psum_scatter(jnp.dot(attended, out_weight, preferred_element_type=jnp...  39.7 us
    sub x2, matrix products, softmax_parts(): weights = jnp.where(keep_mask, jnp.exp(scores - row_top), 0.0)  36.3 us
    all_gather x1, blocking collectives, local(): lax.all_gather(comp_keys, 'ctx', axis=0, tiled=True)  26.6 us
    all_gather x1, blocking collectives, local(): lax.all_gather(comp_values, 'ctx', axis=0, tiled=True)  22.6 us
    dot_general x1, matrix products, local(): jnp.dot(attended, out_weight, preferred_element_type=jnp.float32)  19.5 us
    dot_general x1, matrix products, local(): jnp.einsum('uzai,uix->uzax', selected_weights, tiled_row_groups[..., QUER...  11.4 us
    sub x2, other arithmetic, softmax_parts(): weights = jnp.where(keep_mask, jnp.exp(scores - row_top), 0.0)  11.1 us
    gather x1, local copies, waits for them, and re-layouts, local(): tiled_row_groups = gathered[flat_picks]  9.79 us
  transfers between devices with their start and end apart: 3, of which 1 were waited for; matrix products, arithmetic and copies ran while one was open for 36% of the time, Pallas kernels for 0%

commit v1 on v0

--- a/solution.py
+++ b/solution.py
@@ -67,7 +67,9 @@
         axis=1,
     ).astype(jnp.bfloat16)
     all_comp_keys, all_comp_values = (
-        lax.all_gather(comp_keys, "ctx", axis=0, tiled=True),
+        jnp.concatenate(
+            lax.all_to_all(jnp.stack([comp_keys] * lax.axis_size("ctx")), "ctx", 0, 0), axis=0
+        ),
         lax.all_gather(comp_values, "ctx", axis=0, tiled=True),
     )
     comp_count = all_comp_keys.shape[0]

time: 302 us -> 279 us (0.924)
  blocking collectives: 49.2 us -> 26.5 us
  other arithmetic: 30.4 us -> 22.8 us
  starting transfers between devices: 4.33 us -> 11.4 us
    all_gather x1 -> x0, blocking collectives: 26.6 us -> none  [local(): lax.all_gather(comp_keys, 'ctx', axis=0, tiled=True)]
    all_to_all x0 -> x1, starting transfers between devices: none -> 7.08 us  [local(): lax.all_to_all(jnp.stack([comp_keys] * lax.axis_size('ctx')), 'ctx', 0, 0)]
    all_gather x1, blocking collectives: 22.6 us -> 26.5 us  [local(): lax.all_gather(comp_values, 'ctx', axis=0, tiled=True)]
    unnamed x23 -> x21, local copies, waits for them, and re-layouts: 7.02 us -> 7.06 us
  transfers between devices with their start and end apart: 3 -> 4, of which waited for: 1 -> 1; matrix products, arithmetic and copies ran while one was open for 36% -> 37% of each run, Pallas kernels for 0% -> 0%
where the time goes in v1:
time: 279 us; the launch traced here: 274 us
  matrix products  84.8 us (30%)
  local copies, waits for them, and re-layouts  73.7 us (26%)
  waiting for transfers between devices  39 us (14%)
  blocking collectives  26.5 us (9%)
  other arithmetic  22.8 us (8%)
  between operations  14.2 us (5%)
  starting transfers between devices  11.4 us (4%)
    reduce_scatter x1, waiting for transfers between devices, local(): lax.psum_scatter(jnp.dot(attended, out_weight, preferred_element_type=jnp...  39 us
    sub x2, matrix products, softmax_parts(): weights = jnp.where(keep_mask, jnp.exp(scores - row_top), 0.0)  36.4 us
    all_gather x1, blocking collectives, local(): lax.all_gather(comp_values, 'ctx', axis=0, tiled=True)  26.5 us
    dot_general x1, matrix products, local(): jnp.dot(attended, out_weight, preferred_element_type=jnp.float32)  19.5 us
    dot_general x1, matrix products, local(): jnp.einsum('uzai,uix->uzax', selected_weights, tiled_row_groups[..., QUER...  11.4 us
    sub x2, other arithmetic, softmax_parts(): weights = jnp.where(keep_mask, jnp.exp(scores - row_top), 0.0)  11.1 us
    gather x1, local copies, waits for them, and re-layouts, local(): tiled_row_groups = gathered[flat_picks]  9.79 us
    another operation x4, local copies, waits for them, and re-layouts, local(): jnp.stack([extended[span_index * QBLK:span_index * QBLK + WINDOW + QBLK]...  9.57 us
  transfers between devices with their start and end apart: 4, of which 1 were waited for; matrix products, arithmetic and copies ran while one was open for 37% of the time, Pallas kernels for 0%

profile of v1, /device:TPU:0, one launch (start us, length us, event | category | flops | bytes accessed | tf_op | source)
XLA Modules:
  0.0 273.7 jit_solution(13707045688515047286)
XLA Ops:
  13.0 4.3 %collective-permute-start = (bf16[8,20480]{1,0:T(8,128)(2,1)}, bf16[8,20480]{1,0:T(8,128)(2,1)}, u32[]{:S(2)}, u32[]{:S(2)}) collective-permute-start(bf16[8,20480]{1,0:T(8,128)(2,1)} %slice.53), channel_id=1, source_target_pairs={{0,8},{8,16},{16,24},{24,32},{32,40},{40,48},{48,56},{56,64},{64,7... | collective-permute-start | bytes 983048 | tf_op jit(solution)/shard_map/ppermute | solution.py:21
  19.3 7.1 %all-to-all-start = ((bf16[16,32,192]{2,1,0:T(8,128)(2,1)}), bf16[16,32,192]{2,1,0:T(8,128)(2,1)}, u32[]{:S(2)}, u32[]{:S(2)}) async-start(bf16[16,32,192]{2,1,0:T(8,128)(2,1)} %stack.12), calls=%async_computation | async-start | bytes 524288 | tf_op jit(solution)/shard_map/all_to_all | solution.py:71
  33.1 3.3 %compare_and_fusion = pred[4,256,1024]{1,2,0:T(8,128)(4,1)} fusion(s32[4,256]{1,0:T(4,128)S(1)} %add_add_fusion, s32[4,1024]{1,0:T(4,128)S(1)} %broadcast_add_fusion, pred[4,1024]{1,0:T(4,128)(4,1)S(1)} %and.51), kind=kLoop, calls=%fused_computation.55 | loop fusion | flops 2097152 | bytes 1073152 | tf_op jit(solution)/shard_map/and | solution.py:152
  36.4 3.2 %copy.50 = bf16[1024,1536]{0,1:T(8,128)(2,1)S(1)} copy(bf16[1024,1536]{1,0:T(8,128)(2,1)} %param.10) | data formatting | bytes 6291456 | tf_op args[0]
  39.7 4.0 %reshape.235 = bf16[4,256,8,192]{1,0,3,2:T(4,128)(2,1)} reshape(bf16[1024,1536]{0,1:T(8,128)(2,1)S(1)} %copy.50) | data formatting | bytes 6291456 | tf_op jit(solution)/shard_map/reshape | solution.py:52
  48.9 26.5 %all_gather.6 = bf16[512,128]{1,0:T(8,128)(2,1)} all-gather(bf16[32,128]{1,0:T(8,128)(2,1)S(1)} %multiply_reduce_fusion.1), channel_id=1, replica_groups=mesh['ctx'=16,'head'=8] {'ctx'}, dimensions={0}, use_global_device_ids=true | all-gather | bytes 139264 | tf_op jit(solution)/shard_map/all_gather | solution.py:73
  78.6 28.9 %while.11 = (s32[]{:T(128)}, f32[2,512,8,128]{3,2,1,0:T(8,128)}, s32[2]{0:T(128)S(1)}, s32[1024]{0:T(1024)S(1)}, bf16[1024,8,192]{0,2,1:T(8,128)(2,1)S(1)}, /*in...) while((s32[]{:T(128)}, f32[2,512,8,128]{3,2,1,0:T(8,128)}, ...), condition=%wide.region_5.6_spmd.clone, body=%wide.region_2.5_spmd.clone.sunk | while | flops 1357649920 | bytes 34482888 | solution.py:96
  81.5 5.5 %fusion.113 = (f32[512,8]{0,1:T(8,128)S(1)}, bf16[512,8,512]{0,2,1:T(8,128)(2,1)}) fusion(f32[512,8,512]{0,2,1:T(8,128)S(1)} %fusion.112, pred[512,512]{0,1:T(8,128)(4,1)S(1)} %broadcast_compare_fusion.3), kind=kOutput, calls=%fused_computation.122.clone.1 | output fusion | flops 14680575 | bytes 12861440 | tf_op jit(solution)/shard_map/while/body/eval_jaxpr/sub | solution.py:26
  87.1 3.4 %divide_bitcast_fusion.2 = f32[1,512,8,128]{3,1,2,0:T(8,128)S(1)} fusion(bf16[512,8,512]{0,2,1:T(8,128)(2,1)} %get-tuple-element.158, f32[512,8]{0,1:T(8,128)S(1)} %broadcast_maximum_fusion.2, bf16[512,128]{1,0:T(8,128)(2,1)S(1)} %copy-done.7), kind=kOutput, calls=%fused_computation.13.clone.1 | convolution fusion | flops 537395200 | bytes 6438912 | tf_op jit(solution)/shard_map/while/body/eval_jaxpr/thn,nd->thd/dot_general | solution.py:91
  96.0 5.5 %fusion.113 = (f32[512,8]{0,1:T(8,128)S(1)}, bf16[512,8,512]{0,2,1:T(8,128)(2,1)}) fusion(f32[512,8,512]{0,2,1:T(8,128)S(1)} %fusion.112, pred[512,512]{0,1:T(8,128)(4,1)S(1)} %broadcast_compare_fusion.3), kind=kOutput, calls=%fused_computation.122.clone.1 | output fusion | flops 14680575 | bytes 12861440 | tf_op jit(solution)/shard_map/while/body/eval_jaxpr/sub | solution.py:26
  101.5 3.4 %divide_bitcast_fusion.2 = f32[1,512,8,128]{3,1,2,0:T(8,128)S(1)} fusion(bf16[512,8,512]{0,2,1:T(8,128)(2,1)} %get-tuple-element.158, f32[512,8]{0,1:T(8,128)S(1)} %broadcast_maximum_fusion.2, bf16[512,128]{1,0:T(8,128)(2,1)S(1)} %copy-done.7), kind=kOutput, calls=%fused_computation.13.clone.1 | convolution fusion | flops 537395200 | bytes 6438912 | tf_op jit(solution)/shard_map/while/body/eval_jaxpr/thn,nd->thd/dot_general | solution.py:91
  111.0 2.8 %stack.13 = bf16[1,768,320]{2,1,0:T(8,128)(2,1)} reshape(bf16[12,20480]{1,0:T(8,128)(2,1)} %get-tuple-element.96) | data formatting | bytes 983040 | tf_op jit(solution)/shard_map/stack | solution.py:101
  120.6 3.0 %pad_maximum_fusion = bf16[4,768,320]{1,2,0:T(8,128)(2,1)} fusion(bf16[1,768,320]{1,2,0:T(8,128)(2,1)} %get-tuple-element.99, bf16[1,768,320]{1,2,0:T(8,128)(2,1)} %get-tuple-element.98, bf16[1,768,320]{1,2,0:T(8,128)(2,1)} %copy.67, bf16[1,768,320]{1,2,0:T(8,128)(2,1)} %copy.66), kind=kLoop, calls=%fused_computation.68 | loop fusion | flops 2949120 | bytes 3932160 | tf_op jit(solution)/shard_map/stack | solution.py:101
  123.5 15.6 %fusion.88 = (f32[4,256,8]{1,2,0:T(8,128)S(1)}, bf16[4,256,8,768]{1,3,2,0:T(8,128)(2,1)}) fusion(pred[4,256,768]{1,2,0:T(8,128)(4,1)} %compare_and_fusion.1, bf16[4,256,8,192]{1,0,3,2:T(4,128)(2,1)S(1)} %copy-done.3, bf16[4,768,320]{1,2,0:T(8,128)(2,1)} %pad_maximum_fusion), kind=kOutput, calls=%fused_computation.124 | convolution fusion | flops 4875878912 | bytes 22839296 | tf_op jit(solution)/shard_map/sub | solution.py:26
  139.2 7.8 %broadcast_divide_fusion = f32[4,256,8,128]{3,1,2,0:T(8,128)S(1)} fusion(f32[4,256,8]{1,2,0:T(8,128)S(1)} %get-tuple-element.103, bf16[4,256,8,768]{1,3,2,0:T(8,128)(2,1)} %get-tuple-element.104, bf16[1,768,320]{1,2,0:T(8,128)(2,1)} %get-tuple-element.99, bf16[1,768,320]{1,2,0:T(8,128)(2,1)} %get-tuple-element.98, bf16[1,768,320]{1,2,0:T(8,128)(2,1)} %copy.67, ...), kind=kOutput, calls=%fused_computation.61 | convolution fusion | flops 1614807040 | bytes 18776064 | tf_op jit(solution)/shard_map/uzai,uix->uzax/dot_general | solution.py:129
  147.0 4.5 %copy.71 = f32[4,256,8,128]{3,2,1,0:T(8,128)} copy(f32[4,256,8,128]{3,1,2,0:T(8,128)S(1)} %broadcast_divide_fusion) | data formatting | bytes 8388608 | tf_op jit(solution)/shard_map/div | solution.py:129
  151.5 9.8 %gather_fusion = bf16[64,20480]{1,0:T(8,128)(2,1)S(1)} fusion(bf16[256,20480]{1,0:T(8,128)(2,1)} %all-gather.2.cloned.1.call-done, s32[1024]{0:T(1024)S(1)} %pad_clamp_fusion), kind=kCustom, calls=%fused_computation | custom fusion | bytes 5243136 | tf_op jit(solution)/shard_map/gather | solution.py:140
  161.3 4.7 %reshape.234 = bf16[4,1024,320]{2,1,0:T(8,128)(2,1)} reshape(bf16[64,20480]{1,0:T(8,128)(2,1)S(1)} %gather_fusion) | data formatting | bytes 5242880 | tf_op jit(solution)/shard_map/reshape | solution.py:141
  166.0 20.7 %fusion.93 = (f32[4,256,8]{1,2,0:T(8,128)S(1)}, bf16[4,256,8,1024]{1,3,2,0:T(8,128)(2,1)}) fusion(pred[4,256,1024]{1,2,0:T(8,128)(4,1)} %compare_and_fusion, bf16[4,256,8,192]{1,0,3,2:T(4,128)(2,1)} %reshape.235, bf16[4,1024,320]{2,1,0:T(8,128)(2,1)} %reshape.234), kind=kOutput, calls=%fused_computation.125 | convolution fusion | flops 6501172224 | bytes 29392896 | tf_op jit(solution)/shard_map/sub | solution.py:26
  186.7 11.4 %fusion.46 = f32[4,256,8,128]{3,1,2,0:T(8,128)S(1)} fusion(bf16[4,256,8,1024]{1,3,2,0:T(8,128)(2,1)} %get-tuple-element.106, f32[4,256,8]{1,2,0:T(8,128)S(1)} %get-tuple-element.105, bf16[4,1024,320]{2,1,0:T(8,128)(2,1)} %reshape.234), kind=kOutput, calls=%fused_computation.58 | convolution fusion | flops 2148532224 | bytes 22052864 | tf_op jit(solution)/shard_map/uzai,uix->uzax/dot_general | solution.py:164
  198.1 4.4 %copy.63 = f32[4,256,8,128]{3,2,1,0:T(8,128)} copy(f32[4,256,8,128]{3,1,2,0:T(8,128)S(1)} %fusion.46) | data formatting | bytes 8388608 | tf_op jit(solution)/shard_map/div | solution.py:164
  204.9 3.0 %mul.146 = f32[1024,8,128]{2,1,0:T(8,128)} broadcast(f32[1024,8]{1,0:T(8,128)S(1)} %copy-done.6), dimensions={0,1} | broadcast | bytes 4227072 | tf_op jit(solution)/shard_map/mul | solution.py:175
  207.9 19.5 %convolution_convert_fusion = bf16[1024,2560]{1,0:T(8,128)(2,1)} fusion(bf16[1024,2560]{1,0:T(8,128)(2,1)} %param.17, f32[128,8,8,128]{3,2,1,0:T(8,128)} %bitcast.148, f32[128,8,8,128]{3,2,1,0:T(8,128)} %bitcast.147, f32[128,8,8,128]{3,2,1,0:T(8,128)} %bitcast.149, f32[128,8,8,128]{3,2,1,0:T(8,128)S(1)} %bitcast.146, f32[128,8,8,128]{3,2,1,0:T(8,128)} %bitcast.33, ...), kind=kOutput, calls=%fused_computation.48 | convolution fusion | flops 5377622016 | bytes 35651584 | tf_op jit(solution)/shard_map/dot_general | solution.py:179
  227.4 39.0 %reduce-scatter.2.cloned.1.call-done = bf16[128,2560]{1,0:T(8,128)(2,1)} async-done(((bf16[1024,2560]{1,0:T(8,128)(2,1)}), bf16[128,2560]{1,0:T(8,128)(2,1)}) %reduce-scatter.2.cloned.1.call-update) | async-done | bytes 655376 | tf_op jit(solution)/shard_map/reduce_scatter | solution.py:178
  (98 shorter events, 45.8 us)
Async XLA Ops:
  6.5 1.4 copy-start
  6.5 145.0 %all-gather.2.cloned.1.call-start = ((), (), s32[]{:S(2)}) async-start(), calls=%async_computation.2 | async-start | bytes 11141120 | tf_op jit(solution)/shard_map/all_gather | solution.py:139
  9.5 26.9 %copy-start.2 = (bf16[1024,128]{0,1:T(8,128)(2,1)}, bf16[1024,128]{0,1:T(8,128)(2,1)S(1)}, u32[]{:S(2)}) copy-start(bf16[1024,128]{0,1:T(8,128)(2,1)S(1)} %copy.84) | copy-start | bytes 786436
  11.6 18.6 %copy-start.8 = (f32[1024,3,8]{0,2,1:T(8,128)S(1)}, f32[1024,3,8]{0,2,1:T(8,128)}, u32[]{:S(2)}) copy-start(f32[1024,3,8]{0,2,1:T(8,128)} %param.16) | copy-start | bytes 294916
  13.0 94.6 %collective-permute-start = (bf16[8,20480]{1,0:T(8,128)(2,1)}, bf16[8,20480]{1,0:T(8,128)(2,1)}, u32[]{:S(2)}, u32[]{:S(2)}) collective-permute-start(bf16[8,20480]{1,0:T(8,128)(2,1)} %slice.53), channel_id=1, source_target_pairs={{0,8},{8,16},{16,24},{24,32},{32,40},{40,48},{48,56},{56,64},{64,7... | collective-permute-start | bytes 983048 | tf_op jit(solution)/shard_map/ppermute | solution.py:21
  19.3 58.2 %all-to-all-start = ((bf16[16,32,192]{2,1,0:T(8,128)(2,1)}), bf16[16,32,192]{2,1,0:T(8,128)(2,1)}, u32[]{:S(2)}, u32[]{:S(2)}) async-start(bf16[16,32,192]{2,1,0:T(8,128)(2,1)} %stack.12), calls=%async_computation | async-start | bytes 524288 | tf_op jit(solution)/shard_map/all_to_all | solution.py:71
  26.4 240.0 %reduce-scatter.2.cloned.1.call-start = ((), (), s32[]{:S(2)}) async-start(), calls=%async_computation.3 | async-start | bytes 5898240 | tf_op jit(solution)/shard_map/reduce_scatter | solution.py:178
  81.5 5.5 %copy-start.7 = (bf16[512,128]{1,0:T(8,128)(2,1)S(1)}, bf16[512,128]{1,0:T(8,128)(2,1)}, u32[]{:S(2)}) copy-start(bf16[512,128]{1,0:T(8,128)(2,1)} %get-tuple-element.188) | copy-start | bytes 393220 | tf_op jit(solution)/shard_map/while
  96.0 5.5 %copy-start.7 = (bf16[512,128]{1,0:T(8,128)(2,1)S(1)}, bf16[512,128]{1,0:T(8,128)(2,1)}, u32[]{:S(2)}) copy-start(bf16[512,128]{1,0:T(8,128)(2,1)} %get-tuple-element.188) | copy-start | bytes 393220 | tf_op jit(solution)/shard_map/while
  111.0 12.5 %copy-start.3 = (bf16[4,256,8,192]{1,0,3,2:T(4,128)(2,1)S(1)}, bf16[4,256,8,192]{1,0,3,2:T(4,128)(2,1)}, u32[]{:S(2)}) copy-start(bf16[4,256,8,192]{1,0,3,2:T(4,128)(2,1)} %reshape.235) | copy-start | bytes 9437188
  198.1 4.5 %copy-start.4 = (f32[1024,8]{1,0:T(8,128)S(1)}, f32[1024,8]{1,0:T(8,128)}, u32[]{:S(2)}) copy-start(f32[1024,8]{1,0:T(8,128)} %copy.49) | copy-start | bytes 98308
  202.6 1.1 copy-start.5
  202.6 2.3 copy-start.6
  207.9 58.5 %copy-start.1 = (bf16[1024,768]{1,0:T(8,128)(2,1)S(1)}, bf16[1024,768]{1,0:T(8,128)(2,1)}, u32[]{:S(2)}) copy-start(bf16[1024,768]{1,0:T(8,128)(2,1)} %param.11) | copy-start | bytes 4718596
Sparse Core Ops, SparseCore 0:
  11.7 86.4 all-gather.1
  227.5 38.8 reduce-scatter.1
